TPU v7x, 32 devices: a whole 2x2x4 slice. The times are simulated.
32 devices in a mesh: groups: 2 (over y), section: 4 (over z), dp: 4 (over x, core).
Axes of the slice: x: 2, y: 2, z: 4, core: 2. Of those that a mesh axis runs over, the one named last changes fastest.
Arguments:
- stream_in: bfloat16 [1152, 3072], P(('groups', 'dp')), parts along dimension 0, may hold values from -6 to 6
- out_grad: bfloat16 [1152, 3072], P(('groups', 'dp')), parts along dimension 0, may hold values from -6 to 6
- mask_blocks: int32 [24, 3, 3], P(('groups', 'dp')), parts along dimension 0, may hold values from 0 to 2, as said below
- norm_gain: float32 [4, 3072], P('section'), may hold values from 0.4 to 1.6
- w_joined: bfloat16 [4, 3072, 1664], P('section', 'dp'), may hold values from -0.109375 to 0.109375
- w_out: bfloat16 [4, 1536, 3072], P('section', 'dp'), may hold values from -0.15625 to 0.15625
Outputs:
- grad_joined: float32 [8, 3072, 1664], P(('groups', 'section'), 'dp'), parts along dimension 0
- grad_out: float32 [8, 1536, 3072], P(('groups', 'section'), 'dp'), parts along dimension 0
- gain_grad: float32 [8, 3072], P(('groups', 'section')), parts along dimension 0
There are 2 independent parts, one for each index of `groups`. A program takes and returns all parts, laid end to end along the dimension named above; an argument that names none is the same for every part. Nothing has to cross between parts.
Inputs may be any that keep to these rules, and one draw needn't show every extreme that they name: `mask_blocks`: entry 0 of the list of query block i is i itself.
All inputs are finite; a program needn't handle non-finite values.
Results may differ from a plain program's by a relative error of at most 0.024.
Values may be sent and summed in bfloat16 or wider, within the bound.
A program may use at most 128 MiB of HBM per device.

v0:
```python
import jax
import jax.numpy as jnp
from jax import lax
from jax.sharding import PartitionSpec as P

NUM_HEADS = 24
HEAD_DIM = 64
BLOCK_LEN = 16
EPSILON = 1e-05


def from_behind(value, axis, steps):
    count = lax.axis_size(axis)
    initial, last = (max(0, -steps), min(count, count - steps))
    return lax.ppermute(value, axis, [(source, source + steps) for source in range(initial, last)])


def allowed_tokens(links, block_len):
    count = links.shape[1]
    block_hits = links[:, :, :, None] == jnp.arange(count, dtype=jnp.int32)[None, None, None, :]
    blocks = jnp.any(block_hits, axis=2)
    return jnp.repeat(jnp.repeat(blocks, block_len, axis=1), block_len, axis=2)


def normalize(stream, gain_row):
    stream_wide = stream.astype(jnp.float32)
    inv_rms = lax.rsqrt(jnp.mean(stream_wide * stream_wide, axis=-1, keepdims=True) + EPSILON)
    normed = (stream_wide * inv_rms * gain_row).astype(jnp.bfloat16)
    return (stream_wide, inv_rms, normed)


def project(normed, weight):
    batch_size, length, model_width = normed.shape
    flat = jnp.dot(normed.reshape(-1, model_width), weight, preferred_element_type=jnp.float32)
    return flat.astype(jnp.bfloat16).reshape(batch_size, length, weight.shape[1])


def attend(joined_rows, allowed):
    batch_size, length, _ = joined_rows.shape
    inner_width = NUM_HEADS * HEAD_DIM
    queries = joined_rows[:, :, :inner_width].reshape(batch_size, length, NUM_HEADS, HEAD_DIM)
    key_rows = joined_rows[:, :, inner_width : inner_width + HEAD_DIM]
    values = joined_rows[:, :, inner_width + HEAD_DIM :]
    scores = jnp.einsum(
        "bihd,bjd->bhij", queries, key_rows, preferred_element_type=jnp.float32
    ) * HEAD_DIM ** (-0.5)
    scores = jnp.where(allowed[:, None], scores, -1e30)
    row_max = jnp.max(scores, axis=-1, keepdims=True)
    exp_scores = jnp.exp(scores - row_max)
    attn_probs = exp_scores / jnp.sum(exp_scores, axis=-1, keepdims=True)
    probs_half = attn_probs.astype(jnp.bfloat16)
    mixed_heads = jnp.einsum(
        "bhij,bjd->bihd", probs_half, values, preferred_element_type=jnp.float32
    )
    mixed_heads = mixed_heads.astype(jnp.bfloat16).reshape(batch_size, length, inner_width)
    return (queries, key_rows, values, attn_probs, probs_half, mixed_heads)


def layer_forward(stream, gain_row, w_joined, w_out, allowed):
    stream_wide, inv_rms, normed = normalize(stream, gain_row)
    joined_rows = project(normed, w_joined)
    _, _, _, attn_probs, _, mixed_heads = attend(joined_rows, allowed)
    batch_size, length, model_width = stream.shape
    update = jnp.dot(
        mixed_heads.reshape(-1, mixed_heads.shape[2]), w_out, preferred_element_type=jnp.float32
    )
    result = (stream_wide + update.reshape(batch_size, length, model_width)).astype(jnp.bfloat16)
    return (result, normed, joined_rows, attn_probs, mixed_heads)


def layer_backward(stream, gain_row, joined_rows, attn_probs, w_joined, w_out, upstream):
    batch_size, length, model_width = stream.shape
    inner_width = NUM_HEADS * HEAD_DIM
    stream_wide = stream.astype(jnp.float32)
    inv_rms = lax.rsqrt(jnp.mean(stream_wide * stream_wide, axis=-1, keepdims=True) + EPSILON)
    queries = joined_rows[:, :, :inner_width].reshape(batch_size, length, NUM_HEADS, HEAD_DIM)
    key_rows = joined_rows[:, :, inner_width : inner_width + HEAD_DIM]
    values = joined_rows[:, :, inner_width + HEAD_DIM :]
    probs_half = attn_probs.astype(jnp.bfloat16)
    grad_mixed = lax.dot_general(
        upstream.reshape(-1, model_width),
        w_out,
        (((1,), (1,)), ((), ())),
        preferred_element_type=jnp.float32,
    )
    grad_mixed = grad_mixed.astype(jnp.bfloat16).reshape(batch_size, length, NUM_HEADS, HEAD_DIM)
    grad_probs = jnp.einsum(
        "bihd,bjd->bhij", grad_mixed, values, preferred_element_type=jnp.float32
    )
    grad_values = jnp.einsum(
        "bhij,bihd->bjd", probs_half, grad_mixed, preferred_element_type=jnp.float32
    )
    inner_sum = jnp.sum(attn_probs * grad_probs, axis=-1, keepdims=True)
    grad_scores = (attn_probs * (grad_probs - inner_sum) * HEAD_DIM ** (-0.5)).astype(jnp.bfloat16)
    grad_queries = jnp.einsum(
        "bhij,bjd->bihd", grad_scores, key_rows, preferred_element_type=jnp.float32
    )
    grad_keys = jnp.einsum(
        "bhij,bihd->bjd", grad_scores, queries, preferred_element_type=jnp.float32
    )
    grad_joined_rows = jnp.concatenate(
        [grad_queries.reshape(batch_size, length, inner_width), grad_keys, grad_values], axis=-1
    ).astype(jnp.bfloat16)
    grad_normed = lax.dot_general(
        grad_joined_rows.reshape(-1, grad_joined_rows.shape[2]),
        w_joined,
        (((1,), (1,)), ((), ())),
        preferred_element_type=jnp.float32,
    )
    grad_normed = grad_normed.reshape(batch_size, length, model_width)
    gained = grad_normed * gain_row
    grad_stream = inv_rms * gained - stream_wide * inv_rms**3 * jnp.mean(
        stream_wide * gained, axis=-1, keepdims=True
    )
    down_grad = (upstream.astype(jnp.float32) + grad_stream).astype(jnp.bfloat16)
    gain_part = jnp.sum((grad_normed * stream_wide * inv_rms).reshape(-1, model_width), axis=0)
    return (down_grad, grad_joined_rows, gain_part)


def pick(stack, index):
    return lax.dynamic_index_in_dim(stack, index, 0, keepdims=False)


def gather_weights(w_joined, w_out):
    return (
        lax.all_gather(w_joined[0], "dp", axis=0, tiled=True),
        lax.all_gather(w_out[0], "dp", axis=0, tiled=True),
    )


def share_columns(rows):
    n = lax.axis_size("dp")
    me = lax.axis_index("dp")
    slots, length, total = rows.shape
    width = total // n
    taken = jnp.zeros((slots, n, length, width), rows.dtype)
    for shift in range(n):
        target = lax.rem(me + shift, n)
        piece = lax.dynamic_slice_in_dim(rows, target * width, width, 2)
        if shift:
            piece = lax.ppermute(piece, "dp", [(i, (i + shift) % n) for i in range(n)])
        source = lax.rem(me + n - shift, n)
        taken = lax.dynamic_update_slice_in_dim(taken, piece[:, None], source, 1)
    return taken


def body(stream_in, out_grad, mask_blocks, norm_gain, w_joined, w_out):
    full_joined, full_out = gather_weights(w_joined, w_out)
    gain_row = norm_gain[0]
    sections = lax.axis_size("section")
    section_index = lax.axis_index("section")
    micro_count = mask_blocks.shape[0]
    model_width = stream_in.shape[1]
    length = stream_in.shape[0] // micro_count
    inputs = stream_in.reshape(micro_count, 1, length, model_width)
    upstreams = out_grad.reshape(micro_count, 1, length, model_width)
    allowed = allowed_tokens(mask_blocks, BLOCK_LEN).reshape(micro_count, 1, length, length)
    step_count = micro_count + sections - 1

    def forward_step(step, state):
        incoming, kept = state
        slot = step - section_index
        active = jnp.logical_and(slot >= 0, slot < micro_count)
        group_index = jnp.clip(slot, 0, micro_count - 1)
        source = jnp.where(section_index == 0, pick(inputs, group_index), incoming)
        result, normed, joined_rows, attn_probs, mixed_heads = layer_forward(
            source, gain_row, full_joined, full_out, pick(allowed, group_index)
        )
        place = jnp.where(active, group_index, micro_count)
        values = (source, joined_rows, attn_probs, normed, mixed_heads)
        kept = tuple(
            (
                lax.dynamic_update_index_in_dim(store, value, place, 0)
                for store, value in zip(kept, values)
            )
        )
        return (from_behind(result, "section", 1), kept)

    def store_of(*shape, dtype=jnp.bfloat16):
        return jnp.zeros((micro_count + 1,) + shape, dtype)

    joined_width = full_joined.shape[1]
    inner_width = full_out.shape[0]
    rest = jnp.zeros((1, length, model_width), jnp.bfloat16)
    kept = (
        store_of(1, length, model_width),
        store_of(1, length, joined_width),
        store_of(1, NUM_HEADS, length, length, dtype=jnp.float32),
        store_of(1, length, model_width),
        store_of(1, length, inner_width),
    )
    _, kept = lax.fori_loop(0, step_count, forward_step, (rest, kept))
    sources, joineds, probs, normeds, mixeds = kept
    columns_normed = share_columns(normeds[:micro_count, 0])
    columns_mixed = share_columns(mixeds[:micro_count, 0])
    behind = sections - 1 - section_index
    replicas = lax.axis_size("dp")

    def place_of(slot):
        return jnp.where(jnp.logical_and(slot >= 0, slot < micro_count), slot, micro_count)

    def backward_step(step, state):
        incoming, last_rows, all_upstream, all_joined, gain_sum = state
        slot = step - behind
        active = jnp.logical_and(slot >= 0, slot < micro_count)
        group_index = jnp.clip(slot, 0, micro_count - 1)
        upstream = jnp.where(section_index == sections - 1, pick(upstreams, group_index), incoming)
        shared_upstream = lax.all_gather(upstream[0], "dp", axis=0)
        shared_joined = lax.all_gather(last_rows, "dp", axis=0)
        down_grad, grad_joined_rows, gain_part = layer_backward(
            pick(sources, group_index),
            gain_row,
            pick(joineds, group_index),
            pick(probs, group_index),
            full_joined,
            full_out,
            upstream,
        )
        all_upstream = lax.dynamic_update_index_in_dim(
            all_upstream, shared_upstream, place_of(slot), 0
        )
        all_joined = lax.dynamic_update_index_in_dim(
            all_joined, shared_joined, place_of(slot - 1), 0
        )
        gain_sum = gain_sum + jnp.where(active, gain_part, 0.0)
        incoming = from_behind(down_grad, "section", -1)
        return (incoming, grad_joined_rows[0], all_upstream, all_joined, gain_sum)

    start_back = (
        rest,
        jnp.zeros((length, joined_width), jnp.bfloat16),
        store_of(replicas, length, model_width),
        store_of(replicas, length, joined_width),
        jnp.zeros((model_width,), jnp.float32),
    )
    _, last_rows, all_upstream, all_joined, gain_sum = lax.fori_loop(
        0, step_count, backward_step, start_back
    )
    all_joined = lax.dynamic_update_index_in_dim(
        all_joined, lax.all_gather(last_rows, "dp", axis=0), place_of(step_count - 1 - behind), 0
    )
    gain_total = jnp.sum(lax.all_gather(gain_sum, "dp", axis=0), axis=0)
    valid_upstream = all_upstream[:micro_count]
    valid_joined = all_joined[:micro_count]

    def flat(rows):
        return rows.reshape(-1, rows.shape[-1])

    over_rows = (((0,), (0,)), ((), ()))
    grad_joined = lax.dot_general(
        flat(columns_normed), flat(valid_joined), over_rows, preferred_element_type=jnp.float32
    )
    grad_output = lax.dot_general(
        flat(columns_mixed), flat(valid_upstream), over_rows, preferred_element_type=jnp.float32
    )
    return (grad_joined[None], grad_output[None], gain_total[None])


def solution(mesh):
    return jax.shard_map(
        body,
        mesh=mesh,
        in_specs=(
            P(("groups", "dp"), None),
            P(("groups", "dp"), None),
            P(("groups", "dp"), None, None),
            P("section", None),
            P("section", "dp", None),
            P("section", "dp", None),
        ),
        out_specs=(
            P(("groups", "section"), "dp", None),
            P(("groups", "section"), "dp", None),
            P(("groups", "section"), None),
        ),
        check_vma=False,
    )
```

profile of v0, /device:TPU:0, one launch (start us, length us, event | category | flops | bytes accessed | tf_op | source)
XLA Modules:
  0.0 662.7 jit_solution(814957823230022412)
XLA Ops:
  9.2 67.4 %all-gather.14.cloned.1.call-done = bf16[1,1536,3072]{2,1,0:T(8,128)(2,1)} async-done(((bf16[1,384,3072]{2,1,0:T(8,128)(2,1)}), bf16[1,1536,3072]{2,1,0:T(8,128)(2,1)}) %all-gather.14.cloned.1.call-update) | async-done | bytes 9437200 | tf_op jit(solution)/shard_map/all_gather | solution.py:127
  76.5 70.3 %all-gather.12.cloned.1.call-done = bf16[1,3072,1664]{2,1,0:T(8,128)(2,1)} async-done(((bf16[1,768,1664]{2,1,0:T(8,128)(2,1)}), bf16[1,3072,1664]{2,1,0:T(8,128)(2,1)}) %all-gather.12.cloned.1.call-update) | async-done | bytes 10223632 | tf_op jit(solution)/shard_map/all_gather | solution.py:126
  152.4 185.4 %while.48 = (s32[]{:T(128)}, bf16[1,48,3072]{2,1,0:T(8,128)(2,1)}, bf16[4,1,48,3072]{3,2,1,0:T(8,128)(2,1)}, bf16[4,1,48,1664]{3,2,1,0:T(8,128)(2,1)}, f32[4,1,2...) while((s32[]{:T(128)}, bf16[1,48,3072]{2,1,0:T(8,128)(2,1)}, ...), condition=%wide.region_5.6_spmd, body=%wide.region_1.5_spmd.sunk | while | flops 960790336 | bytes 28933956 | solution.py:192
  250.1 6.5 bitcast_dynamic-update-slice_fusion.17
  280.6 6.5 bitcast_dynamic-update-slice_fusion.17
  310.8 6.5 bitcast_dynamic-update-slice_fusion.17
  348.5 270.0 %while.49 = (s32[]{:T(128)}, bf16[1,48,3072]{2,1,0:T(8,128)(2,1)}, bf16[48,1664]{1,0:T(8,128)(2,1)S(1)}, bf16[4,4,48,3072]{3,2,1,0:T(8,128)(2,1)}, bf16[4,4,48,1...) while((s32[]{:T(128)}, bf16[1,48,3072]{2,1,0:T(8,128)(2,1)}, ...), condition=%wide.region_11.12_spmd.clone, body=%wide.region_6.11_spmd.clone.sunk | while | flops 975469632 | bytes 40366604 | solution.py:236
  351.3 6.8 %convolution_convert_fusion.5 = bf16[48,1536]{1,0:T(8,128)(2,1)S(1)} fusion(bf16[1536,3072]{1,0:T(8,128)(2,1)} %get-tuple-element.1081, bf16[1,48,3072]{2,1,0:T(8,128)(2,1)} %bitcast_select_fusion.4), kind=kOutput, calls=%fused_computation.31.clone.1 | convolution fusion | flops 453058560 | bytes 9879552 | tf_op jit(solution)/shard_map/while/body/eval_jaxpr/dot_general | solution.py:80
  365.2 7.8 %all-gather.7 = bf16[192,1664]{1,0:T(8,128)(2,1)S(1)} all-gather(bf16[48,1664]{1,0:T(8,128)(2,1)S(1)} %get-tuple-element.1050), channel_id=2, replica_groups=mesh['groups'=2,'section'=4,'dp'=4] {'dp'}, dimensions={0}, use_global_device_ids=true | all-gather | bytes 798720 | tf_op jit(solution)/shard_map/while/body/eval_jaxpr/all_gather | solution.py:209
  373.1 7.2 %fusion.106 = (f32[3072]{0:T(1024)S(1)}, f32[48]{0:T(128)S(1)}, f32[48,3072]{1,0:T(8,128)S(1)}) fusion(f32[48]{0:T(128)S(1)} %get-tuple-element.966, bf16[4,1,48,3072]{3,2,1,0:T(8,128)(2,1)} %get-tuple-element.1078, s32[]{:T(128)S(6)} %min.23, f32[3072]{0:T(1024)S(1)} %bitcast.279, bf16[48,1664]{1,0:T(8,128)(2,1)S(1)} %concatenate.21, ...), kind=kOutput, calls=%fused_computation.52.clone.1 | convolution fusion | flops 491762624 | bytes 11293060 | tf_op jit(solution)/shard_map/while/body/eval_jaxpr/dot_general | solution.py:104
  387.0 7.3 %collective-permute-done.1 = bf16[1,48,3072]{2,1,0:T(8,128)(2,1)} collective-permute-done((bf16[1,48,3072]{2,1,0:T(8,128)(2,1)}, bf16[1,48,3072]{2,1,0:T(8,128)(2,1)}, u32[]{:S(2)}, u32[]{:S(2)}) %collective-permute-start.1) | collective-permute-done | bytes 294944 | tf_op jit(solution)/shard_map/while/body/eval_jaxpr/ppermute | solution.py:15
  397.1 6.8 %convolution_convert_fusion.5 = bf16[48,1536]{1,0:T(8,128)(2,1)S(1)} fusion(bf16[1536,3072]{1,0:T(8,128)(2,1)} %get-tuple-element.1081, bf16[1,48,3072]{2,1,0:T(8,128)(2,1)} %bitcast_select_fusion.4), kind=kOutput, calls=%fused_computation.31.clone.1 | convolution fusion | flops 453058560 | bytes 9879552 | tf_op jit(solution)/shard_map/while/body/eval_jaxpr/dot_general | solution.py:80
  411.0 7.3 %all-gather.7 = bf16[192,1664]{1,0:T(8,128)(2,1)S(1)} all-gather(bf16[48,1664]{1,0:T(8,128)(2,1)S(1)} %get-tuple-element.1050), channel_id=2, replica_groups=mesh['groups'=2,'section'=4,'dp'=4] {'dp'}, dimensions={0}, use_global_device_ids=true | all-gather | bytes 798720 | tf_op jit(solution)/shard_map/while/body/eval_jaxpr/all_gather | solution.py:209
  418.5 7.2 %fusion.106 = (f32[3072]{0:T(1024)S(1)}, f32[48]{0:T(128)S(1)}, f32[48,3072]{1,0:T(8,128)S(1)}) fusion(f32[48]{0:T(128)S(1)} %get-tuple-element.966, bf16[4,1,48,3072]{3,2,1,0:T(8,128)(2,1)} %get-tuple-element.1078, s32[]{:T(128)S(6)} %min.23, f32[3072]{0:T(1024)S(1)} %bitcast.279, bf16[48,1664]{1,0:T(8,128)(2,1)S(1)} %concatenate.21, ...), kind=kOutput, calls=%fused_computation.52.clone.1 | convolution fusion | flops 491762624 | bytes 11293060 | tf_op jit(solution)/shard_map/while/body/eval_jaxpr/dot_general | solution.py:104
  432.3 6.8 %collective-permute-done.1 = bf16[1,48,3072]{2,1,0:T(8,128)(2,1)} collective-permute-done((bf16[1,48,3072]{2,1,0:T(8,128)(2,1)}, bf16[1,48,3072]{2,1,0:T(8,128)(2,1)}, u32[]{:S(2)}, u32[]{:S(2)}) %collective-permute-start.1) | collective-permute-done | bytes 294944 | tf_op jit(solution)/shard_map/while/body/eval_jaxpr/ppermute | solution.py:15
  441.9 6.8 %convolution_convert_fusion.5 = bf16[48,1536]{1,0:T(8,128)(2,1)S(1)} fusion(bf16[1536,3072]{1,0:T(8,128)(2,1)} %get-tuple-element.1081, bf16[1,48,3072]{2,1,0:T(8,128)(2,1)} %bitcast_select_fusion.4), kind=kOutput, calls=%fused_computation.31.clone.1 | convolution fusion | flops 453058560 | bytes 9879552 | tf_op jit(solution)/shard_map/while/body/eval_jaxpr/dot_general | solution.py:80
  455.9 7.3 %all-gather.7 = bf16[192,1664]{1,0:T(8,128)(2,1)S(1)} all-gather(bf16[48,1664]{1,0:T(8,128)(2,1)S(1)} %get-tuple-element.1050), channel_id=2, replica_groups=mesh['groups'=2,'section'=4,'dp'=4] {'dp'}, dimensions={0}, use_global_device_ids=true | all-gather | bytes 798720 | tf_op jit(solution)/shard_map/while/body/eval_jaxpr/all_gather | solution.py:209
  463.3 7.2 %fusion.106 = (f32[3072]{0:T(1024)S(1)}, f32[48]{0:T(128)S(1)}, f32[48,3072]{1,0:T(8,128)S(1)}) fusion(f32[48]{0:T(128)S(1)} %get-tuple-element.966, bf16[4,1,48,3072]{3,2,1,0:T(8,128)(2,1)} %get-tuple-element.1078, s32[]{:T(128)S(6)} %min.23, f32[3072]{0:T(1024)S(1)} %bitcast.279, bf16[48,1664]{1,0:T(8,128)(2,1)S(1)} %concatenate.21, ...), kind=kOutput, calls=%fused_computation.52.clone.1 | convolution fusion | flops 491762624 | bytes 11293060 | tf_op jit(solution)/shard_map/while/body/eval_jaxpr/dot_general | solution.py:104
  477.1 6.8 %collective-permute-done.1 = bf16[1,48,3072]{2,1,0:T(8,128)(2,1)} collective-permute-done((bf16[1,48,3072]{2,1,0:T(8,128)(2,1)}, bf16[1,48,3072]{2,1,0:T(8,128)(2,1)}, u32[]{:S(2)}, u32[]{:S(2)}) %collective-permute-start.1) | collective-permute-done | bytes 294944 | tf_op jit(solution)/shard_map/while/body/eval_jaxpr/ppermute | solution.py:15
  486.8 6.8 %convolution_convert_fusion.5 = bf16[48,1536]{1,0:T(8,128)(2,1)S(1)} fusion(bf16[1536,3072]{1,0:T(8,128)(2,1)} %get-tuple-element.1081, bf16[1,48,3072]{2,1,0:T(8,128)(2,1)} %bitcast_select_fusion.4), kind=kOutput, calls=%fused_computation.31.clone.1 | convolution fusion | flops 453058560 | bytes 9879552 | tf_op jit(solution)/shard_map/while/body/eval_jaxpr/dot_general | solution.py:80
  500.7 7.3 %all-gather.7 = bf16[192,1664]{1,0:T(8,128)(2,1)S(1)} all-gather(bf16[48,1664]{1,0:T(8,128)(2,1)S(1)} %get-tuple-element.1050), channel_id=2, replica_groups=mesh['groups'=2,'section'=4,'dp'=4] {'dp'}, dimensions={0}, use_global_device_ids=true | all-gather | bytes 798720 | tf_op jit(solution)/shard_map/while/body/eval_jaxpr/all_gather | solution.py:209
  508.2 7.2 %fusion.106 = (f32[3072]{0:T(1024)S(1)}, f32[48]{0:T(128)S(1)}, f32[48,3072]{1,0:T(8,128)S(1)}) fusion(f32[48]{0:T(128)S(1)} %get-tuple-element.966, bf16[4,1,48,3072]{3,2,1,0:T(8,128)(2,1)} %get-tuple-element.1078, s32[]{:T(128)S(6)} %min.23, f32[3072]{0:T(1024)S(1)} %bitcast.279, bf16[48,1664]{1,0:T(8,128)(2,1)S(1)} %concatenate.21, ...), kind=kOutput, calls=%fused_computation.52.clone.1 | convolution fusion | flops 491762624 | bytes 11293060 | tf_op jit(solution)/shard_map/while/body/eval_jaxpr/dot_general | solution.py:104
  522.0 6.8 %collective-permute-done.1 = bf16[1,48,3072]{2,1,0:T(8,128)(2,1)} collective-permute-done((bf16[1,48,3072]{2,1,0:T(8,128)(2,1)}, bf16[1,48,3072]{2,1,0:T(8,128)(2,1)}, u32[]{:S(2)}, u32[]{:S(2)}) %collective-permute-start.1) | collective-permute-done | bytes 294944 | tf_op jit(solution)/shard_map/while/body/eval_jaxpr/ppermute | solution.py:15
  531.6 6.8 %convolution_convert_fusion.5 = bf16[48,1536]{1,0:T(8,128)(2,1)S(1)} fusion(bf16[1536,3072]{1,0:T(8,128)(2,1)} %get-tuple-element.1081, bf16[1,48,3072]{2,1,0:T(8,128)(2,1)} %bitcast_select_fusion.4), kind=kOutput, calls=%fused_computation.31.clone.1 | convolution fusion | flops 453058560 | bytes 9879552 | tf_op jit(solution)/shard_map/while/body/eval_jaxpr/dot_general | solution.py:80
  545.6 7.3 %all-gather.7 = bf16[192,1664]{1,0:T(8,128)(2,1)S(1)} all-gather(bf16[48,1664]{1,0:T(8,128)(2,1)S(1)} %get-tuple-element.1050), channel_id=2, replica_groups=mesh['groups'=2,'section'=4,'dp'=4] {'dp'}, dimensions={0}, use_global_device_ids=true | all-gather | bytes 798720 | tf_op jit(solution)/shard_map/while/body/eval_jaxpr/all_gather | solution.py:209
  553.0 7.2 %fusion.106 = (f32[3072]{0:T(1024)S(1)}, f32[48]{0:T(128)S(1)}, f32[48,3072]{1,0:T(8,128)S(1)}) fusion(f32[48]{0:T(128)S(1)} %get-tuple-element.966, bf16[4,1,48,3072]{3,2,1,0:T(8,128)(2,1)} %get-tuple-element.1078, s32[]{:T(128)S(6)} %min.23, f32[3072]{0:T(1024)S(1)} %bitcast.279, bf16[48,1664]{1,0:T(8,128)(2,1)S(1)} %concatenate.21, ...), kind=kOutput, calls=%fused_computation.52.clone.1 | convolution fusion | flops 491762624 | bytes 11293060 | tf_op jit(solution)/shard_map/while/body/eval_jaxpr/dot_general | solution.py:104
  566.8 6.9 %collective-permute-done.1 = bf16[1,48,3072]{2,1,0:T(8,128)(2,1)} collective-permute-done((bf16[1,48,3072]{2,1,0:T(8,128)(2,1)}, bf16[1,48,3072]{2,1,0:T(8,128)(2,1)}, u32[]{:S(2)}, u32[]{:S(2)}) %collective-permute-start.1) | collective-permute-done | bytes 294944 | tf_op jit(solution)/shard_map/while/body/eval_jaxpr/ppermute | solution.py:15
  576.5 6.8 %convolution_convert_fusion.5 = bf16[48,1536]{1,0:T(8,128)(2,1)S(1)} fusion(bf16[1536,3072]{1,0:T(8,128)(2,1)} %get-tuple-element.1081, bf16[1,48,3072]{2,1,0:T(8,128)(2,1)} %bitcast_select_fusion.4), kind=kOutput, calls=%fused_computation.31.clone.1 | convolution fusion | flops 453058560 | bytes 9879552 | tf_op jit(solution)/shard_map/while/body/eval_jaxpr/dot_general | solution.py:80
  590.4 7.3 %all-gather.7 = bf16[192,1664]{1,0:T(8,128)(2,1)S(1)} all-gather(bf16[48,1664]{1,0:T(8,128)(2,1)S(1)} %get-tuple-element.1050), channel_id=2, replica_groups=mesh['groups'=2,'section'=4,'dp'=4] {'dp'}, dimensions={0}, use_global_device_ids=true | all-gather | bytes 798720 | tf_op jit(solution)/shard_map/while/body/eval_jaxpr/all_gather | solution.py:209
  597.9 7.2 %fusion.106 = (f32[3072]{0:T(1024)S(1)}, f32[48]{0:T(128)S(1)}, f32[48,3072]{1,0:T(8,128)S(1)}) fusion(f32[48]{0:T(128)S(1)} %get-tuple-element.966, bf16[4,1,48,3072]{3,2,1,0:T(8,128)(2,1)} %get-tuple-element.1078, s32[]{:T(128)S(6)} %min.23, f32[3072]{0:T(1024)S(1)} %bitcast.279, bf16[48,1664]{1,0:T(8,128)(2,1)S(1)} %concatenate.21, ...), kind=kOutput, calls=%fused_computation.52.clone.1 | convolution fusion | flops 491762624 | bytes 11293060 | tf_op jit(solution)/shard_map/while/body/eval_jaxpr/dot_general | solution.py:104
  611.7 6.8 %collective-permute-done.1 = bf16[1,48,3072]{2,1,0:T(8,128)(2,1)} collective-permute-done((bf16[1,48,3072]{2,1,0:T(8,128)(2,1)}, bf16[1,48,3072]{2,1,0:T(8,128)(2,1)}, u32[]{:S(2)}, u32[]{:S(2)}) %collective-permute-start.1) | collective-permute-done | bytes 294944 | tf_op jit(solution)/shard_map/while/body/eval_jaxpr/ppermute | solution.py:15
  618.5 8.6 %all-gather.3 = bf16[192,1664]{1,0:T(8,128)(2,1)S(1)} all-gather(bf16[48,1664]{1,0:T(8,128)(2,1)S(1)} %get-tuple-element.640), channel_id=5, replica_groups=mesh['groups'=2,'section'=4,'dp'=4] {'dp'}, dimensions={0}, use_global_device_ids=true | all-gather | bytes 798720 | tf_op jit(solution)/shard_map/all_gather | solution.py:240
  (451 shorter events, 310.9 us)
Async XLA Ops:
  7.2 69.4 %all-gather.14.cloned.1.call-start = ((), (), s32[]{:S(2)}) async-start(), calls=%async_computation.1 | async-start | bytes 11796480 | tf_op jit(solution)/shard_map/all_gather | solution.py:127
  7.9 138.9 %all-gather.12.cloned.1.call-start = ((), (), s32[]{:S(2)}) async-start(), calls=%async_computation | async-start | bytes 12779520 | tf_op jit(solution)/shard_map/all_gather | solution.py:126
  173.6 10.5 %collective-permute-start = (bf16[1,48,3072]{2,1,0:T(8,128)(2,1)}, bf16[1,48,3072]{2,1,0:T(8,128)(2,1)}, u32[]{:S(2)}, u32[]{:S(2)}) collective-permute-start(bf16[1,48,3072]{2,1,0:T(8,128)(2,1)} %fusion.90), channel_id=1, source_target_pairs={{0,4},{4,8},{8,12},{1,5},{5,9},{9,13},{2,6},{6,10},{10,14},{3,7},{... | collective-permute-start | bytes 884744 | tf_op jit(solution)/shard_map/while/body/eval_jaxpr/ppermute | solution.py:15
  205.3 10.6 %collective-permute-start = (bf16[1,48,3072]{2,1,0:T(8,128)(2,1)}, bf16[1,48,3072]{2,1,0:T(8,128)(2,1)}, u32[]{:S(2)}, u32[]{:S(2)}) collective-permute-start(bf16[1,48,3072]{2,1,0:T(8,128)(2,1)} %fusion.90), channel_id=1, source_target_pairs={{0,4},{4,8},{8,12},{1,5},{5,9},{9,13},{2,6},{6,10},{10,14},{3,7},{... | collective-permute-start | bytes 884744 | tf_op jit(solution)/shard_map/while/body/eval_jaxpr/ppermute | solution.py:15
  237.1 9.7 %collective-permute-start = (bf16[1,48,3072]{2,1,0:T(8,128)(2,1)}, bf16[1,48,3072]{2,1,0:T(8,128)(2,1)}, u32[]{:S(2)}, u32[]{:S(2)}) collective-permute-start(bf16[1,48,3072]{2,1,0:T(8,128)(2,1)} %fusion.90), channel_id=1, source_target_pairs={{0,4},{4,8},{8,12},{1,5},{5,9},{9,13},{2,6},{6,10},{10,14},{3,7},{... | collective-permute-start | bytes 884744 | tf_op jit(solution)/shard_map/while/body/eval_jaxpr/ppermute | solution.py:15
  268.1 9.3 %collective-permute-start = (bf16[1,48,3072]{2,1,0:T(8,128)(2,1)}, bf16[1,48,3072]{2,1,0:T(8,128)(2,1)}, u32[]{:S(2)}, u32[]{:S(2)}) collective-permute-start(bf16[1,48,3072]{2,1,0:T(8,128)(2,1)} %fusion.90), channel_id=1, source_target_pairs={{0,4},{4,8},{8,12},{1,5},{5,9},{9,13},{2,6},{6,10},{10,14},{3,7},{... | collective-permute-start | bytes 884744 | tf_op jit(solution)/shard_map/while/body/eval_jaxpr/ppermute | solution.py:15
  298.6 9.0 %collective-permute-start = (bf16[1,48,3072]{2,1,0:T(8,128)(2,1)}, bf16[1,48,3072]{2,1,0:T(8,128)(2,1)}, u32[]{:S(2)}, u32[]{:S(2)}) collective-permute-start(bf16[1,48,3072]{2,1,0:T(8,128)(2,1)} %fusion.90), channel_id=1, source_target_pairs={{0,4},{4,8},{8,12},{1,5},{5,9},{9,13},{2,6},{6,10},{10,14},{3,7},{... | collective-permute-start | bytes 884744 | tf_op jit(solution)/shard_map/while/body/eval_jaxpr/ppermute | solution.py:15
  328.8 9.0 %collective-permute-start = (bf16[1,48,3072]{2,1,0:T(8,128)(2,1)}, bf16[1,48,3072]{2,1,0:T(8,128)(2,1)}, u32[]{:S(2)}, u32[]{:S(2)}) collective-permute-start(bf16[1,48,3072]{2,1,0:T(8,128)(2,1)} %fusion.90), channel_id=1, source_target_pairs={{0,4},{4,8},{8,12},{1,5},{5,9},{9,13},{2,6},{6,10},{10,14},{3,7},{... | collective-permute-start | bytes 884744 | tf_op jit(solution)/shard_map/while/body/eval_jaxpr/ppermute | solution.py:15
  340.1 310.2 %collective-permute-start.4 = (bf16[3,48,768]{2,1,0:T(8,128)(2,1)}, bf16[3,48,768]{2,1,0:T(8,128)(2,1)}, u32[]{:S(2)}, u32[]{:S(2)}) collective-permute-start(bf16[3,48,768]{2,1,0:T(8,128)(2,1)} %get-tuple-element.763), channel_id=1, source_target_pairs={{0,3},{1,0},{2,1},{3,2},{4,7},{5,4},{6,5},{7,6},{8,11},{9,8},{10,9... | collective-permute-start | bytes 663560 | tf_op jit(solution)/shard_map/ppermute | solution.py:141
  340.1 309.2 %collective-permute-start.3 = (bf16[3,48,768]{2,1,0:T(8,128)(2,1)}, bf16[3,48,768]{2,1,0:T(8,128)(2,1)}, u32[]{:S(2)}, u32[]{:S(2)}) collective-permute-start(bf16[3,48,768]{2,1,0:T(8,128)(2,1)} %get-tuple-element.764), channel_id=1, source_target_pairs={{0,2},{1,3},{2,0},{3,1},{4,6},{5,7},{6,4},{7,5},{8,10},{9,11},{10,... | collective-permute-start | bytes 663560 | tf_op jit(solution)/shard_map/ppermute | solution.py:141
  340.6 307.7 %collective-permute-start.2 = (bf16[3,48,768]{2,1,0:T(8,128)(2,1)}, bf16[3,48,768]{2,1,0:T(8,128)(2,1)}, u32[]{:S(2)}, u32[]{:S(2)}) collective-permute-start(bf16[3,48,768]{2,1,0:T(8,128)(2,1)} %get-tuple-element.765), channel_id=1, source_target_pairs={{0,1},{1,2},{2,3},{3,0},{4,5},{5,6},{6,7},{7,4},{8,9},{9,10},{10,1... | collective-permute-start | bytes 663560 | tf_op jit(solution)/shard_map/ppermute | solution.py:141
  341.7 298.5 %collective-permute-start.7 = (bf16[3,48,384]{2,1,0:T(8,128)(2,1)}, bf16[3,48,384]{2,1,0:T(8,128)(2,1)}, u32[]{:S(2)}, u32[]{:S(2)}) collective-permute-start(bf16[3,48,384]{2,1,0:T(8,128)(2,1)} %get-tuple-element.767), channel_id=1, source_target_pairs={{0,3},{1,0},{2,1},{3,2},{4,7},{5,4},{6,5},{7,6},{8,11},{9,8},{10,9... | collective-permute-start | bytes 331784 | tf_op jit(solution)/shard_map/ppermute | solution.py:141
  348.5 36.1 %all-gather.16.cloned.1.call-start = ((), (), s32[]{:S(2)}) async-start(), calls=%async_computation.2 | async-start | bytes 1474560 | tf_op jit(solution)/shard_map/while/body/eval_jaxpr/all_gather | solution.py:208
  373.1 10.5 %copy-start.13 = (f32[3072]{0:T(1024)S(1)}, f32[3072]{0:T(1024)}, u32[]{:S(2)}) copy-start(f32[3072]{0:T(1024)} %get-tuple-element.1053) | copy-start | bytes 36868 | tf_op jit(solution)/shard_map/while
  382.3 11.9 %collective-permute-start.1 = (bf16[1,48,3072]{2,1,0:T(8,128)(2,1)}, bf16[1,48,3072]{2,1,0:T(8,128)(2,1)}, u32[]{:S(2)}, u32[]{:S(2)}) collective-permute-start(bf16[1,48,3072]{2,1,0:T(8,128)(2,1)} %fusion.107), channel_id=1, source_target_pairs={{4,0},{8,4},{12,8},{5,1},{9,5},{13,9},{6,2},{10,6},{14,10},{7,3},{... | collective-permute-start | bytes 884744 | tf_op jit(solution)/shard_map/while/body/eval_jaxpr/ppermute | solution.py:15
  383.7 10.6 %copy-start.14 = (f32[3072]{0:T(1024)}, f32[3072]{0:T(1024)S(1)}, u32[]{:S(2)}) copy-start(f32[3072]{0:T(1024)S(1)} %select_add_fusion.2) | copy-start | bytes 36868 | tf_op jit(solution)/shard_map/while
  394.2 35.7 %all-gather.16.cloned.1.call-start = ((), (), s32[]{:S(2)}) async-start(), calls=%async_computation.2 | async-start | bytes 1474560 | tf_op jit(solution)/shard_map/while/body/eval_jaxpr/all_gather | solution.py:208
  418.4 10.5 %copy-start.13 = (f32[3072]{0:T(1024)S(1)}, f32[3072]{0:T(1024)}, u32[]{:S(2)}) copy-start(f32[3072]{0:T(1024)} %get-tuple-element.1053) | copy-start | bytes 36868 | tf_op jit(solution)/shard_map/while
  427.6 11.5 %collective-permute-start.1 = (bf16[1,48,3072]{2,1,0:T(8,128)(2,1)}, bf16[1,48,3072]{2,1,0:T(8,128)(2,1)}, u32[]{:S(2)}, u32[]{:S(2)}) collective-permute-start(bf16[1,48,3072]{2,1,0:T(8,128)(2,1)} %fusion.107), channel_id=1, source_target_pairs={{4,0},{8,4},{12,8},{5,1},{9,5},{13,9},{6,2},{10,6},{14,10},{7,3},{... | collective-permute-start | bytes 884744 | tf_op jit(solution)/shard_map/while/body/eval_jaxpr/ppermute | solution.py:15
  439.1 35.6 %all-gather.16.cloned.1.call-start = ((), (), s32[]{:S(2)}) async-start(), calls=%async_computation.2 | async-start | bytes 1474560 | tf_op jit(solution)/shard_map/while/body/eval_jaxpr/all_gather | solution.py:208
  463.3 10.5 %copy-start.13 = (f32[3072]{0:T(1024)S(1)}, f32[3072]{0:T(1024)}, u32[]{:S(2)}) copy-start(f32[3072]{0:T(1024)} %get-tuple-element.1053) | copy-start | bytes 36868 | tf_op jit(solution)/shard_map/while
  472.5 11.5 %collective-permute-start.1 = (bf16[1,48,3072]{2,1,0:T(8,128)(2,1)}, bf16[1,48,3072]{2,1,0:T(8,128)(2,1)}, u32[]{:S(2)}, u32[]{:S(2)}) collective-permute-start(bf16[1,48,3072]{2,1,0:T(8,128)(2,1)} %fusion.107), channel_id=1, source_target_pairs={{4,0},{8,4},{12,8},{5,1},{9,5},{13,9},{6,2},{10,6},{14,10},{7,3},{... | collective-permute-start | bytes 884744 | tf_op jit(solution)/shard_map/while/body/eval_jaxpr/ppermute | solution.py:15
  483.9 35.7 %all-gather.16.cloned.1.call-start = ((), (), s32[]{:S(2)}) async-start(), calls=%async_computation.2 | async-start | bytes 1474560 | tf_op jit(solution)/shard_map/while/body/eval_jaxpr/all_gather | solution.py:208
  508.2 10.5 %copy-start.13 = (f32[3072]{0:T(1024)S(1)}, f32[3072]{0:T(1024)}, u32[]{:S(2)}) copy-start(f32[3072]{0:T(1024)} %get-tuple-element.1053) | copy-start | bytes 36868 | tf_op jit(solution)/shard_map/while
  517.3 11.5 %collective-permute-start.1 = (bf16[1,48,3072]{2,1,0:T(8,128)(2,1)}, bf16[1,48,3072]{2,1,0:T(8,128)(2,1)}, u32[]{:S(2)}, u32[]{:S(2)}) collective-permute-start(bf16[1,48,3072]{2,1,0:T(8,128)(2,1)} %fusion.107), channel_id=1, source_target_pairs={{4,0},{8,4},{12,8},{5,1},{9,5},{13,9},{6,2},{10,6},{14,10},{7,3},{... | collective-permute-start | bytes 884744 | tf_op jit(solution)/shard_map/while/body/eval_jaxpr/ppermute | solution.py:15
  528.8 35.6 %all-gather.16.cloned.1.call-start = ((), (), s32[]{:S(2)}) async-start(), calls=%async_computation.2 | async-start | bytes 1474560 | tf_op jit(solution)/shard_map/while/body/eval_jaxpr/all_gather | solution.py:208
  562.2 11.5 %collective-permute-start.1 = (bf16[1,48,3072]{2,1,0:T(8,128)(2,1)}, bf16[1,48,3072]{2,1,0:T(8,128)(2,1)}, u32[]{:S(2)}, u32[]{:S(2)}) collective-permute-start(bf16[1,48,3072]{2,1,0:T(8,128)(2,1)} %fusion.107), channel_id=1, source_target_pairs={{4,0},{8,4},{12,8},{5,1},{9,5},{13,9},{6,2},{10,6},{14,10},{7,3},{... | collective-permute-start | bytes 884744 | tf_op jit(solution)/shard_map/while/body/eval_jaxpr/ppermute | solution.py:15
  573.6 35.7 %all-gather.16.cloned.1.call-start = ((), (), s32[]{:S(2)}) async-start(), calls=%async_computation.2 | async-start | bytes 1474560 | tf_op jit(solution)/shard_map/while/body/eval_jaxpr/all_gather | solution.py:208
  597.8 10.5 %copy-start.13 = (f32[3072]{0:T(1024)S(1)}, f32[3072]{0:T(1024)}, u32[]{:S(2)}) copy-start(f32[3072]{0:T(1024)} %get-tuple-element.1053) | copy-start | bytes 36868 | tf_op jit(solution)/shard_map/while
  607.0 11.5 %collective-permute-start.1 = (bf16[1,48,3072]{2,1,0:T(8,128)(2,1)}, bf16[1,48,3072]{2,1,0:T(8,128)(2,1)}, u32[]{:S(2)}, u32[]{:S(2)}) collective-permute-start(bf16[1,48,3072]{2,1,0:T(8,128)(2,1)} %fusion.107), channel_id=1, source_target_pairs={{4,0},{8,4},{12,8},{5,1},{9,5},{13,9},{6,2},{10,6},{14,10},{7,3},{... | collective-permute-start | bytes 884744 | tf_op jit(solution)/shard_map/while/body/eval_jaxpr/ppermute | solution.py:15
  618.5 15.6 %collective-permute-start.5 = (bf16[3,48,384]{2,1,0:T(8,128)(2,1)}, bf16[3,48,384]{2,1,0:T(8,128)(2,1)S(1)}, u32[]{:S(2)}, u32[]{:S(2)}) collective-permute-start(bf16[3,48,384]{2,1,0:T(8,128)(2,1)} %get-tuple-element.769), channel_id=1, source_target_pairs={{0,1},{1,2},{2,3},{3,0},{4,5},{5,6},{6,7},{7,4},{8,9},{9,10},{10,1... | collective-permute-start | bytes 331784 | tf_op jit(solution)/shard_map/ppermute | solution.py:141
  634.1 5.5 collective-permute-start.6
  (67 other events, 363.4 us)
Sparse Core Ops, SparseCore 0:
  9.6 66.9 all-gather.13
  78.1 68.6 all-gather.11
  350.9 19.0 all-gather.15
  396.3 16.7 all-gather.15
  441.2 17.1 all-gather.15
  486.0 17.0 all-gather.15
  531.2 17.2 all-gather.15
  576.0 17.0 all-gather.15
where the time goes:
time: 667 us; the launch traced here: 663 us
  matrix products  208 us (31%)
  waiting for transfers between devices  188 us (28%)
  local copies, waits for them, and re-layouts  90.4 us (14%)
  other arithmetic  60.8 us (9%)
  blocking collectives  58.4 us (9%)
  starting transfers between devices  40.5 us (6%)
  between operations  14.3 us (2%)
    all_gather x1, waiting for transfers between devices, gather_weights(): lax.all_gather(w_joined[0], 'dp', axis=0, tiled=True)  70.3 us
    all_gather x1, waiting for transfers between devices, gather_weights(): lax.all_gather(w_out[0], 'dp', axis=0, tiled=True)  67.4 us
    ppermute x12, waiting for transfers between devices, from_behind(): lax.ppermute(value, axis, [(source, source + steps) for source in range(i...  45.4 us
    all_gather x6, blocking collectives, backward_step(): shared_joined = lax.all_gather(last_rows, 'dp', axis=0)  44.4 us
    dot_general x6, matrix products, layer_backward(): lax.dot_general(grad_joined_rows.reshape(-1, grad_joined_rows.shape[2]),...  43.3 us
    dot_general x6, matrix products, layer_backward(): lax.dot_general(upstream.reshape(-1, model_width), w_out, (((1,), (1,)),...  40.7 us
    dot_general x6, matrix products, project(): jnp.dot(normed.reshape(-1, model_width), weight, preferred_element_type=j...  39.1 us
    dot_general x6, matrix products, layer_forward(): jnp.dot(mixed_heads.reshape(-1, mixed_heads.shape[2]), w_out, preferred_e...  37.3 us
  transfers between devices with their start and end apart: 26, of which 12 were waited for; matrix products, arithmetic and copies ran while one was open for 33% of the time, Pallas kernels for 0%

commit v1 on v0

--- a/solution.py
+++ b/solution.py
@@ -2,11 +2,36 @@
 import jax.numpy as jnp
 from jax import lax
 from jax.sharding import PartitionSpec as P
+from jax.lax import axis_index, axis_size, ppermute
 
 NUM_HEADS = 24
 HEAD_DIM = 64
 BLOCK_LEN = 16
 EPSILON = 1e-05
+
+
+def _follow_local_data(inp, d0):
+    inp = jnp.moveaxis(inp, 0, d0)
+    plain = inp.shape
+    return inp.reshape(*plain[:d0], plain[d0] * plain[d0 + 1], *plain[d0 + 2 :])
+
+
+def search_outputs(block_in, named_axis, dim_at):
+    amount_of = axis_size(named_axis)
+    copies = tuple(((dd, (dd + 1) % amount_of) for dd in range(amount_of)))
+    found = tuple(((dev_j, nth) for nth, dev_j in copies))
+    p_next, lower = ([], [])
+    d = 0
+    while d < amount_of - 1:
+        if d % 2 == 0:
+            p_next.append(ppermute(p_next[-1] if p_next else block_in, named_axis, copies))
+        else:
+            lower.append(ppermute(lower[-1] if lower else block_in, named_axis, found))
+        d += 1
+    kept_arr = jnp.stack([*p_next[::-1], block_in, *lower], axis=0)
+    all_rows = axis_index(named_axis) - len(p_next)
+    kept_arr = kept_arr[(jnp.arange(amount_of) - all_rows) % amount_of]
+    return _follow_local_data(kept_arr, dim_at)
 
 
 def from_behind(value, axis, steps):
@@ -123,7 +148,7 @@
 
 def gather_weights(w_joined, w_out):
     return (
-        lax.all_gather(w_joined[0], "dp", axis=0, tiled=True),
+        search_outputs(w_joined[0], "dp", 0),
         lax.all_gather(w_out[0], "dp", axis=0, tiled=True),
     )
 

time: 667 us -> 690 us (1.034)
  local copies, waits for them, and re-layouts: 90.4 us -> 109 us
  waiting for transfers between devices: 188 us -> 170 us
  blocking collectives: 58.4 us -> 76 us
  matrix products: 208 us -> 192 us
  starting transfers between devices: 40.5 us -> 51.6 us
  other arithmetic: 60.8 us -> 71.3 us
    ppermute x0 -> x3, waiting for transfers between devices: none -> 126 us  [the longest x2 126 us: search_outputs(): ppermute(p_next[-1] if p_next else block_in, named_axis, copies)]
    all_gather x1 -> x0, waiting for transfers between devices: 70.3 us -> none  [gather_weights(): lax.all_gather(w_joined[0], 'dp', axis=0, tiled=True)]
    all_gather x1, waiting for transfers between devices: 67.4 us -> 0.01 us  [gather_weights(): lax.all_gather(w_out[0], 'dp', axis=0, tiled=True)]
    all_gather x6, blocking collectives: 44.4 us -> 63.7 us  [backward_step(): shared_joined = lax.all_gather(last_rows, 'dp', axis=0)]
    gather x0 -> x3, local copies, waits for them, and re-layouts: none -> 14.4 us  [search_outputs(): kept_arr = kept_arr[(jnp.arange(amount_of) - all_rows) % amount_of]]
    ppermute x0 -> x3, starting transfers between devices: none -> 9.68 us  [the longest x2 7.69 us: search_outputs(): ppermute(p_next[-1] if p_next else block_in, named_axis, copies)]
    unnamed x1 -> x2, other arithmetic: 0.01 us -> 9.39 us
    dot_general x6, matrix products: 10.7 us -> 2.85 us  [layer_backward(): jnp.einsum('bihd,bjd->bhij', grad_mixed, values, preferred_element_type=j...]
  transfers between devices with their start and end apart: 26 -> 28, of which waited for: 12 -> 10; matrix products, arithmetic and copies ran while one was open for 33% -> 34% of each run, Pallas kernels for 0% -> 0%
where the time goes in v1:
time: 690 us; the launch traced here: 685 us
  matrix products  192 us (28%)
  waiting for transfers between devices  170 us (25%)
  local copies, waits for them, and re-layouts  109 us (16%)
  blocking collectives  76 us (11%)
  other arithmetic  71.3 us (10%)
  starting transfers between devices  51.6 us (7%)
  between operations  14.2 us (2%)
    ppermute x2, waiting for transfers between devices, search_outputs(): ppermute(p_next[-1] if p_next else block_in, named_axis, copies)  126 us
    all_gather x6, blocking collectives, backward_step(): shared_joined = lax.all_gather(last_rows, 'dp', axis=0)  63.7 us
    dot_general x6, matrix products, layer_backward(): lax.dot_general(grad_joined_rows.reshape(-1, grad_joined_rows.shape[2]),...  43.3 us
    ppermute x12, waiting for transfers between devices, from_behind(): lax.ppermute(value, axis, [(source, source + steps) for source in range(i...  41.3 us
    dot_general x6, matrix products, layer_backward(): lax.dot_general(upstream.reshape(-1, model_width), w_out, (((1,), (1,)),...  40.4 us
    dot_general x6, matrix products, project(): jnp.dot(normed.reshape(-1, model_width), weight, preferred_element_type=j...  39 us
    ppermute x12, starting transfers between devices, from_behind(): lax.ppermute(value, axis, [(source, source + steps) for source in range(i...  37.6 us
    dot_general x6, matrix products, layer_forward(): jnp.dot(mixed_heads.reshape(-1, mixed_heads.shape[2]), w_out, preferred_e...  37.4 us
  transfers between devices with their start and end apart: 28, of which 10 were waited for; matrix products, arithmetic and copies ran while one was open for 34% of the time, Pallas kernels for 0%

profile of v1, /device:TPU:0, one launch (start us, length us, event | category | flops | bytes accessed | tf_op | source)
XLA Modules:
  0.0 685.2 jit_solution(4823511099581338566)
XLA Ops:
  10.4 93.1 %collective-permute-done.2 = bf16[768,1664]{1,0:T(8,128)(2,1)S(1)} collective-permute-done((bf16[768,1664]{1,0:T(8,128)(2,1)}, bf16[768,1664]{1,0:T(8,128)(2,1)S(1)}, u32[]{:S(2)}, u32[]{:S(2)}) %collective-permute-start.2) | collective-permute-done | bytes 2555936 | tf_op jit(solution)/shard_map/ppermute | solution.py:27
  103.5 7.2 %collective-permute-start.3 = (bf16[768,1664]{1,0:T(8,128)(2,1)S(1)}, bf16[768,1664]{1,0:T(8,128)(2,1)}, u32[]{:S(2)}, u32[]{:S(2)}) collective-permute-start(bf16[768,1664]{1,0:T(8,128)(2,1)S(1)} %collective-permute-done.2), channel_id=1, source_target_pairs={{0,1},{1,2},{2,3},{3,0},{4,5},{5,6},{6,7},{7,4},{8,9},{9,10},{10,1... | collective-permute-start | bytes 7667720 | tf_op jit(solution)/shard_map/ppermute | solution.py:27
  111.9 32.8 %collective-permute-done.3 = bf16[768,1664]{1,0:T(8,128)(2,1)} collective-permute-done((bf16[768,1664]{1,0:T(8,128)(2,1)S(1)}, bf16[768,1664]{1,0:T(8,128)(2,1)}, u32[]{:S(2)}, u32[]{:S(2)}) %collective-permute-start.3) | collective-permute-done | bytes 2555936 | tf_op jit(solution)/shard_map/ppermute | solution.py:27
  168.1 9.4 %pad_maximum_fusion.1 = bf16[4,768,1664]{2,1,0:T(8,128)(2,1)} fusion(bf16[4,768,768]{2,1,0:T(8,128)(2,1)} %gather_fusion.1, bf16[4,768,896]{2,1,0:T(8,128)(2,1)} %gather_fusion), kind=kLoop, calls=%fused_computation.79 | loop fusion | flops 20447232 | bytes 20447232
  183.1 179.4 %while.48 = (s32[]{:T(128)}, bf16[1,48,3072]{2,1,0:T(8,128)(2,1)}, bf16[4,1,48,3072]{3,2,1,0:T(8,128)(2,1)}, bf16[4,1,48,1664]{3,2,1,0:T(8,128)(2,1)}, f32[4,1,2...) while((s32[]{:T(128)}, bf16[1,48,3072]{2,1,0:T(8,128)(2,1)}, ...), condition=%wide.region_5.6_spmd, body=%wide.region_1.5_spmd.sunk | while | flops 960790336 | bytes 28930116 | solution.py:217
  215.8 6.5 bitcast_dynamic-update-slice_fusion.17
  371.8 272.7 %while.49 = (s32[]{:T(128)}, bf16[1,48,3072]{2,1,0:T(8,128)(2,1)}, bf16[48,1664]{1,0:T(8,128)(2,1)S(1)}, bf16[4,4,48,3072]{3,2,1,0:T(8,128)(2,1)}, bf16[4,4,48,1...) while((s32[]{:T(128)}, bf16[1,48,3072]{2,1,0:T(8,128)(2,1)}, ...), condition=%wide.region_11.12_spmd.clone, body=%wide.region_6.11_spmd.clone.sunk | while | flops 975469632 | bytes 47283840 | solution.py:261
  374.1 6.7 convolution_convert_fusion.5
  383.4 11.6 %all-gather.6 = bf16[192,1664]{1,0:T(8,128)(2,1)S(1)} all-gather(bf16[48,1664]{1,0:T(8,128)(2,1)S(1)} %get-tuple-element.1050), channel_id=2, replica_groups=mesh['groups'=2,'section'=4,'dp'=4] {'dp'}, dimensions={0}, use_global_device_ids=true | all-gather | bytes 798720 | tf_op jit(solution)/shard_map/while/body/eval_jaxpr/all_gather | solution.py:234
  398.3 7.2 %fusion.108 = (f32[3072]{0:T(1024)S(1)}, f32[48]{0:T(128)S(1)}, f32[48,3072]{1,0:T(8,128)S(1)}) fusion(f32[48]{0:T(128)S(1)} %get-tuple-element.966, bf16[4,1,48,3072]{3,2,1,0:T(8,128)(2,1)} %get-tuple-element.1078, s32[]{:T(128)S(6)} %min.23, f32[3072]{0:T(1024)S(1)} %bitcast.289, bf16[48,1664]{1,0:T(8,128)(2,1)S(1)} %concatenate.21, ...), kind=kOutput, calls=%fused_computation.54.clone.1 | convolution fusion | flops 491762624 | bytes 11293060 | tf_op jit(solution)/shard_map/while/body/eval_jaxpr/dot_general | solution.py:129
  411.5 7.2 %collective-permute-done.1 = bf16[1,48,3072]{2,1,0:T(8,128)(2,1)} collective-permute-done((bf16[1,48,3072]{2,1,0:T(8,128)(2,1)S(1)}, bf16[1,48,3072]{2,1,0:T(8,128)(2,1)}, u32[]{:S(2)}, u32[]{:S(2)}) %collective-permute-start.1) | collective-permute-done | bytes 294944 | tf_op jit(solution)/shard_map/while/body/eval_jaxpr/ppermute | solution.py:40
  421.0 6.7 convolution_convert_fusion.5
  430.2 11.2 %all-gather.6 = bf16[192,1664]{1,0:T(8,128)(2,1)S(1)} all-gather(bf16[48,1664]{1,0:T(8,128)(2,1)S(1)} %get-tuple-element.1050), channel_id=2, replica_groups=mesh['groups'=2,'section'=4,'dp'=4] {'dp'}, dimensions={0}, use_global_device_ids=true | all-gather | bytes 798720 | tf_op jit(solution)/shard_map/while/body/eval_jaxpr/all_gather | solution.py:234
  444.8 7.2 %fusion.108 = (f32[3072]{0:T(1024)S(1)}, f32[48]{0:T(128)S(1)}, f32[48,3072]{1,0:T(8,128)S(1)}) fusion(f32[48]{0:T(128)S(1)} %get-tuple-element.966, bf16[4,1,48,3072]{3,2,1,0:T(8,128)(2,1)} %get-tuple-element.1078, s32[]{:T(128)S(6)} %min.23, f32[3072]{0:T(1024)S(1)} %bitcast.289, bf16[48,1664]{1,0:T(8,128)(2,1)S(1)} %concatenate.21, ...), kind=kOutput, calls=%fused_computation.54.clone.1 | convolution fusion | flops 491762624 | bytes 11293060 | tf_op jit(solution)/shard_map/while/body/eval_jaxpr/dot_general | solution.py:129
  458.0 6.6 collective-permute-done.1
  466.9 6.7 convolution_convert_fusion.5
  476.2 10.2 %all-gather.6 = bf16[192,1664]{1,0:T(8,128)(2,1)S(1)} all-gather(bf16[48,1664]{1,0:T(8,128)(2,1)S(1)} %get-tuple-element.1050), channel_id=2, replica_groups=mesh['groups'=2,'section'=4,'dp'=4] {'dp'}, dimensions={0}, use_global_device_ids=true | all-gather | bytes 798720 | tf_op jit(solution)/shard_map/while/body/eval_jaxpr/all_gather | solution.py:234
  489.8 7.2 %fusion.108 = (f32[3072]{0:T(1024)S(1)}, f32[48]{0:T(128)S(1)}, f32[48,3072]{1,0:T(8,128)S(1)}) fusion(f32[48]{0:T(128)S(1)} %get-tuple-element.966, bf16[4,1,48,3072]{3,2,1,0:T(8,128)(2,1)} %get-tuple-element.1078, s32[]{:T(128)S(6)} %min.23, f32[3072]{0:T(1024)S(1)} %bitcast.289, bf16[48,1664]{1,0:T(8,128)(2,1)S(1)} %concatenate.21, ...), kind=kOutput, calls=%fused_computation.54.clone.1 | convolution fusion | flops 491762624 | bytes 11293060 | tf_op jit(solution)/shard_map/while/body/eval_jaxpr/dot_general | solution.py:129
  503.0 6.6 collective-permute-done.1
  511.9 6.7 convolution_convert_fusion.5
  521.2 10.2 %all-gather.6 = bf16[192,1664]{1,0:T(8,128)(2,1)S(1)} all-gather(bf16[48,1664]{1,0:T(8,128)(2,1)S(1)} %get-tuple-element.1050), channel_id=2, replica_groups=mesh['groups'=2,'section'=4,'dp'=4] {'dp'}, dimensions={0}, use_global_device_ids=true | all-gather | bytes 798720 | tf_op jit(solution)/shard_map/while/body/eval_jaxpr/all_gather | solution.py:234
  534.7 7.2 %fusion.108 = (f32[3072]{0:T(1024)S(1)}, f32[48]{0:T(128)S(1)}, f32[48,3072]{1,0:T(8,128)S(1)}) fusion(f32[48]{0:T(128)S(1)} %get-tuple-element.966, bf16[4,1,48,3072]{3,2,1,0:T(8,128)(2,1)} %get-tuple-element.1078, s32[]{:T(128)S(6)} %min.23, f32[3072]{0:T(1024)S(1)} %bitcast.289, bf16[48,1664]{1,0:T(8,128)(2,1)S(1)} %concatenate.21, ...), kind=kOutput, calls=%fused_computation.54.clone.1 | convolution fusion | flops 491762624 | bytes 11293060 | tf_op jit(solution)/shard_map/while/body/eval_jaxpr/dot_general | solution.py:129
  547.9 6.6 collective-permute-done.1
  556.8 6.7 convolution_convert_fusion.5
  566.1 10.2 %all-gather.6 = bf16[192,1664]{1,0:T(8,128)(2,1)S(1)} all-gather(bf16[48,1664]{1,0:T(8,128)(2,1)S(1)} %get-tuple-element.1050), channel_id=2, replica_groups=mesh['groups'=2,'section'=4,'dp'=4] {'dp'}, dimensions={0}, use_global_device_ids=true | all-gather | bytes 798720 | tf_op jit(solution)/shard_map/while/body/eval_jaxpr/all_gather | solution.py:234
  579.7 7.2 %fusion.108 = (f32[3072]{0:T(1024)S(1)}, f32[48]{0:T(128)S(1)}, f32[48,3072]{1,0:T(8,128)S(1)}) fusion(f32[48]{0:T(128)S(1)} %get-tuple-element.966, bf16[4,1,48,3072]{3,2,1,0:T(8,128)(2,1)} %get-tuple-element.1078, s32[]{:T(128)S(6)} %min.23, f32[3072]{0:T(1024)S(1)} %bitcast.289, bf16[48,1664]{1,0:T(8,128)(2,1)S(1)} %concatenate.21, ...), kind=kOutput, calls=%fused_computation.54.clone.1 | convolution fusion | flops 491762624 | bytes 11293060 | tf_op jit(solution)/shard_map/while/body/eval_jaxpr/dot_general | solution.py:129
  592.9 6.7 collective-permute-done.1
  601.8 6.7 convolution_convert_fusion.5
  611.1 10.2 %all-gather.6 = bf16[192,1664]{1,0:T(8,128)(2,1)S(1)} all-gather(bf16[48,1664]{1,0:T(8,128)(2,1)S(1)} %get-tuple-element.1050), channel_id=2, replica_groups=mesh['groups'=2,'section'=4,'dp'=4] {'dp'}, dimensions={0}, use_global_device_ids=true | all-gather | bytes 798720 | tf_op jit(solution)/shard_map/while/body/eval_jaxpr/all_gather | solution.py:234
  624.7 7.2 %fusion.108 = (f32[3072]{0:T(1024)S(1)}, f32[48]{0:T(128)S(1)}, f32[48,3072]{1,0:T(8,128)S(1)}) fusion(f32[48]{0:T(128)S(1)} %get-tuple-element.966, bf16[4,1,48,3072]{3,2,1,0:T(8,128)(2,1)} %get-tuple-element.1078, s32[]{:T(128)S(6)} %min.23, f32[3072]{0:T(1024)S(1)} %bitcast.289, bf16[48,1664]{1,0:T(8,128)(2,1)S(1)} %concatenate.21, ...), kind=kOutput, calls=%fused_computation.54.clone.1 | convolution fusion | flops 491762624 | bytes 11293060 | tf_op jit(solution)/shard_map/while/body/eval_jaxpr/dot_general | solution.py:129
  637.9 6.7 collective-permute-done.1
  644.5 7.1 %all-gather.2 = bf16[192,1664]{1,0:T(8,128)(2,1)S(1)} all-gather(bf16[48,1664]{1,0:T(8,128)(2,1)S(1)} %get-tuple-element.640), channel_id=4, replica_groups=mesh['groups'=2,'section'=4,'dp'=4] {'dp'}, dimensions={0}, use_global_device_ids=true | all-gather | bytes 798720 | tf_op jit(solution)/shard_map/all_gather | solution.py:265
  (400 shorter events, 325.5 us)
Async XLA Ops:
  7.2 170.3 %all-gather.10.cloned.1.call-start = ((), (), s32[]{:S(2)}) async-start(), calls=%async_computation | async-start | bytes 11796480 | tf_op jit(solution)/shard_map/all_gather | solution.py:152
  7.9 95.6 %collective-permute-start.2 = (bf16[768,1664]{1,0:T(8,128)(2,1)}, bf16[768,1664]{1,0:T(8,128)(2,1)S(1)}, u32[]{:S(2)}, u32[]{:S(2)}) collective-permute-start(bf16[768,1664]{1,0:T(8,128)(2,1)} %bitcast.283), channel_id=1, source_target_pairs={{0,1},{1,2},{2,3},{3,0},{4,5},{5,6},{6,7},{7,4},{8,9},{9,10},{10,1... | collective-permute-start | bytes 7667720 | tf_op jit(solution)/shard_map/ppermute | solution.py:27
  8.4 103.4 %collective-permute-start.4 = (bf16[768,1664]{1,0:T(8,128)(2,1)}, bf16[768,1664]{1,0:T(8,128)(2,1)}, u32[]{:S(2)}, u32[]{:S(2)}) collective-permute-start(bf16[768,1664]{1,0:T(8,128)(2,1)} %bitcast.284), channel_id=1, source_target_pairs={{1,0},{2,1},{3,2},{0,3},{5,4},{6,5},{7,6},{4,7},{9,8},{10,9},{11,1... | collective-permute-start | bytes 7667720 | tf_op jit(solution)/shard_map/ppermute | solution.py:29
  103.5 41.1 %collective-permute-start.3 = (bf16[768,1664]{1,0:T(8,128)(2,1)S(1)}, bf16[768,1664]{1,0:T(8,128)(2,1)}, u32[]{:S(2)}, u32[]{:S(2)}) collective-permute-start(bf16[768,1664]{1,0:T(8,128)(2,1)S(1)} %collective-permute-done.2), channel_id=1, source_target_pairs={{0,1},{1,2},{2,3},{3,0},{4,5},{5,6},{6,7},{7,4},{8,9},{9,10},{10,1... | collective-permute-start | bytes 7667720 | tf_op jit(solution)/shard_map/ppermute | solution.py:27
  203.7 10.1 %collective-permute-start = (bf16[1,48,3072]{2,1,0:T(8,128)(2,1)}, bf16[1,48,3072]{2,1,0:T(8,128)(2,1)}, u32[]{:S(2)}, u32[]{:S(2)}) collective-permute-start(bf16[1,48,3072]{2,1,0:T(8,128)(2,1)} %fusion.92), channel_id=1, source_target_pairs={{0,4},{4,8},{8,12},{1,5},{5,9},{9,13},{2,6},{6,10},{10,14},{3,7},{... | collective-permute-start | bytes 884744 | tf_op jit(solution)/shard_map/while/body/eval_jaxpr/ppermute | solution.py:40
  234.5 9.3 %collective-permute-start = (bf16[1,48,3072]{2,1,0:T(8,128)(2,1)}, bf16[1,48,3072]{2,1,0:T(8,128)(2,1)}, u32[]{:S(2)}, u32[]{:S(2)}) collective-permute-start(bf16[1,48,3072]{2,1,0:T(8,128)(2,1)} %fusion.92), channel_id=1, source_target_pairs={{0,4},{4,8},{8,12},{1,5},{5,9},{9,13},{2,6},{6,10},{10,14},{3,7},{... | collective-permute-start | bytes 884744 | tf_op jit(solution)/shard_map/while/body/eval_jaxpr/ppermute | solution.py:40
  264.5 9.3 %collective-permute-start = (bf16[1,48,3072]{2,1,0:T(8,128)(2,1)}, bf16[1,48,3072]{2,1,0:T(8,128)(2,1)}, u32[]{:S(2)}, u32[]{:S(2)}) collective-permute-start(bf16[1,48,3072]{2,1,0:T(8,128)(2,1)} %fusion.92), channel_id=1, source_target_pairs={{0,4},{4,8},{8,12},{1,5},{5,9},{9,13},{2,6},{6,10},{10,14},{3,7},{... | collective-permute-start | bytes 884744 | tf_op jit(solution)/shard_map/while/body/eval_jaxpr/ppermute | solution.py:40
  294.4 9.0 %collective-permute-start = (bf16[1,48,3072]{2,1,0:T(8,128)(2,1)}, bf16[1,48,3072]{2,1,0:T(8,128)(2,1)}, u32[]{:S(2)}, u32[]{:S(2)}) collective-permute-start(bf16[1,48,3072]{2,1,0:T(8,128)(2,1)} %fusion.92), channel_id=1, source_target_pairs={{0,4},{4,8},{8,12},{1,5},{5,9},{9,13},{2,6},{6,10},{10,14},{3,7},{... | collective-permute-start | bytes 884744 | tf_op jit(solution)/shard_map/while/body/eval_jaxpr/ppermute | solution.py:40
  324.0 9.0 %collective-permute-start = (bf16[1,48,3072]{2,1,0:T(8,128)(2,1)}, bf16[1,48,3072]{2,1,0:T(8,128)(2,1)}, u32[]{:S(2)}, u32[]{:S(2)}) collective-permute-start(bf16[1,48,3072]{2,1,0:T(8,128)(2,1)} %fusion.92), channel_id=1, source_target_pairs={{0,4},{4,8},{8,12},{1,5},{5,9},{9,13},{2,6},{6,10},{10,14},{3,7},{... | collective-permute-start | bytes 884744 | tf_op jit(solution)/shard_map/while/body/eval_jaxpr/ppermute | solution.py:40
  353.6 9.0 %collective-permute-start = (bf16[1,48,3072]{2,1,0:T(8,128)(2,1)}, bf16[1,48,3072]{2,1,0:T(8,128)(2,1)}, u32[]{:S(2)}, u32[]{:S(2)}) collective-permute-start(bf16[1,48,3072]{2,1,0:T(8,128)(2,1)} %fusion.92), channel_id=1, source_target_pairs={{0,4},{4,8},{8,12},{1,5},{5,9},{9,13},{2,6},{6,10},{10,14},{3,7},{... | collective-permute-start | bytes 884744 | tf_op jit(solution)/shard_map/while/body/eval_jaxpr/ppermute | solution.py:40
  364.8 306.0 %collective-permute-start.5 = (bf16[3,48,768]{2,1,0:T(8,128)(2,1)}, bf16[3,48,768]{2,1,0:T(8,128)(2,1)}, u32[]{:S(2)}, u32[]{:S(2)}) collective-permute-start(bf16[3,48,768]{2,1,0:T(8,128)(2,1)} %get-tuple-element.765), channel_id=1, source_target_pairs={{0,1},{1,2},{2,3},{3,0},{4,5},{5,6},{6,7},{7,4},{8,9},{9,10},{10,1... | collective-permute-start | bytes 663560 | tf_op jit(solution)/shard_map/ppermute | solution.py:166
  364.8 307.0 %collective-permute-start.6 = (bf16[3,48,768]{2,1,0:T(8,128)(2,1)}, bf16[3,48,768]{2,1,0:T(8,128)(2,1)}, u32[]{:S(2)}, u32[]{:S(2)}) collective-permute-start(bf16[3,48,768]{2,1,0:T(8,128)(2,1)} %get-tuple-element.764), channel_id=1, source_target_pairs={{0,2},{1,3},{2,0},{3,1},{4,6},{5,7},{6,4},{7,5},{8,10},{9,11},{10,... | collective-permute-start | bytes 663560 | tf_op jit(solution)/shard_map/ppermute | solution.py:166
  365.0 307.7 %collective-permute-start.7 = (bf16[3,48,768]{2,1,0:T(8,128)(2,1)}, bf16[3,48,768]{2,1,0:T(8,128)(2,1)}, u32[]{:S(2)}, u32[]{:S(2)}) collective-permute-start(bf16[3,48,768]{2,1,0:T(8,128)(2,1)} %get-tuple-element.763), channel_id=1, source_target_pairs={{0,3},{1,0},{2,1},{3,2},{4,7},{5,4},{6,5},{7,6},{8,11},{9,8},{10,9... | collective-permute-start | bytes 663560 | tf_op jit(solution)/shard_map/ppermute | solution.py:166
  371.8 24.2 %copy-start.1 = (f32[4,1,24,48,48]{3,4,2,1,0:T(8,128)}, f32[4,1,24,48,48]{3,4,2,1,0:T(8,128)S(1)}, u32[]{:S(2)}) copy-start(f32[4,1,24,48,48]{3,4,2,1,0:T(8,128)S(1)} %get-tuple-element.1080) | copy-start | bytes 2654212 | tf_op jit(solution)/shard_map/while
  371.8 37.3 %all-gather.12.cloned.1.call-start = ((), (), s32[]{:S(2)}) async-start(), calls=%async_computation.1 | async-start | bytes 1474560 | tf_op jit(solution)/shard_map/while/body/eval_jaxpr/all_gather | solution.py:233
  406.9 11.8 %collective-permute-start.1 = (bf16[1,48,3072]{2,1,0:T(8,128)(2,1)S(1)}, bf16[1,48,3072]{2,1,0:T(8,128)(2,1)}, u32[]{:S(2)}, u32[]{:S(2)}) collective-permute-start(bf16[1,48,3072]{2,1,0:T(8,128)(2,1)S(1)} %fusion.109), channel_id=1, source_target_pairs={{4,0},{8,4},{12,8},{5,1},{9,5},{13,9},{6,2},{10,6},{14,10},{7,3},{... | collective-permute-start | bytes 884744 | tf_op jit(solution)/shard_map/while/body/eval_jaxpr/ppermute | solution.py:40
  418.7 23.9 %copy-start.1 = (f32[4,1,24,48,48]{3,4,2,1,0:T(8,128)}, f32[4,1,24,48,48]{3,4,2,1,0:T(8,128)S(1)}, u32[]{:S(2)}) copy-start(f32[4,1,24,48,48]{3,4,2,1,0:T(8,128)S(1)} %get-tuple-element.1080) | copy-start | bytes 2654212 | tf_op jit(solution)/shard_map/while
  418.7 36.9 %all-gather.12.cloned.1.call-start = ((), (), s32[]{:S(2)}) async-start(), calls=%async_computation.1 | async-start | bytes 1474560 | tf_op jit(solution)/shard_map/while/body/eval_jaxpr/all_gather | solution.py:233
  453.4 11.3 %collective-permute-start.1 = (bf16[1,48,3072]{2,1,0:T(8,128)(2,1)S(1)}, bf16[1,48,3072]{2,1,0:T(8,128)(2,1)}, u32[]{:S(2)}, u32[]{:S(2)}) collective-permute-start(bf16[1,48,3072]{2,1,0:T(8,128)(2,1)S(1)} %fusion.109), channel_id=1, source_target_pairs={{4,0},{8,4},{12,8},{5,1},{9,5},{13,9},{6,2},{10,6},{14,10},{7,3},{... | collective-permute-start | bytes 884744 | tf_op jit(solution)/shard_map/while/body/eval_jaxpr/ppermute | solution.py:40
  464.7 36.0 %all-gather.12.cloned.1.call-start = ((), (), s32[]{:S(2)}) async-start(), calls=%async_computation.1 | async-start | bytes 1474560 | tf_op jit(solution)/shard_map/while/body/eval_jaxpr/all_gather | solution.py:233
  498.4 11.3 %collective-permute-start.1 = (bf16[1,48,3072]{2,1,0:T(8,128)(2,1)S(1)}, bf16[1,48,3072]{2,1,0:T(8,128)(2,1)}, u32[]{:S(2)}, u32[]{:S(2)}) collective-permute-start(bf16[1,48,3072]{2,1,0:T(8,128)(2,1)S(1)} %fusion.109), channel_id=1, source_target_pairs={{4,0},{8,4},{12,8},{5,1},{9,5},{13,9},{6,2},{10,6},{14,10},{7,3},{... | collective-permute-start | bytes 884744 | tf_op jit(solution)/shard_map/while/body/eval_jaxpr/ppermute | solution.py:40
  509.6 22.9 %copy-start.1 = (f32[4,1,24,48,48]{3,4,2,1,0:T(8,128)}, f32[4,1,24,48,48]{3,4,2,1,0:T(8,128)S(1)}, u32[]{:S(2)}) copy-start(f32[4,1,24,48,48]{3,4,2,1,0:T(8,128)S(1)} %get-tuple-element.1080) | copy-start | bytes 2654212 | tf_op jit(solution)/shard_map/while
  509.6 36.0 %all-gather.12.cloned.1.call-start = ((), (), s32[]{:S(2)}) async-start(), calls=%async_computation.1 | async-start | bytes 1474560 | tf_op jit(solution)/shard_map/while/body/eval_jaxpr/all_gather | solution.py:233
  543.3 11.3 %collective-permute-start.1 = (bf16[1,48,3072]{2,1,0:T(8,128)(2,1)S(1)}, bf16[1,48,3072]{2,1,0:T(8,128)(2,1)}, u32[]{:S(2)}, u32[]{:S(2)}) collective-permute-start(bf16[1,48,3072]{2,1,0:T(8,128)(2,1)S(1)} %fusion.109), channel_id=1, source_target_pairs={{4,0},{8,4},{12,8},{5,1},{9,5},{13,9},{6,2},{10,6},{14,10},{7,3},{... | collective-permute-start | bytes 884744 | tf_op jit(solution)/shard_map/while/body/eval_jaxpr/ppermute | solution.py:40
  554.6 35.9 %all-gather.12.cloned.1.call-start = ((), (), s32[]{:S(2)}) async-start(), calls=%async_computation.1 | async-start | bytes 1474560 | tf_op jit(solution)/shard_map/while/body/eval_jaxpr/all_gather | solution.py:233
  588.3 11.3 %collective-permute-start.1 = (bf16[1,48,3072]{2,1,0:T(8,128)(2,1)S(1)}, bf16[1,48,3072]{2,1,0:T(8,128)(2,1)}, u32[]{:S(2)}, u32[]{:S(2)}) collective-permute-start(bf16[1,48,3072]{2,1,0:T(8,128)(2,1)S(1)} %fusion.109), channel_id=1, source_target_pairs={{4,0},{8,4},{12,8},{5,1},{9,5},{13,9},{6,2},{10,6},{14,10},{7,3},{... | collective-permute-start | bytes 884744 | tf_op jit(solution)/shard_map/while/body/eval_jaxpr/ppermute | solution.py:40
  599.5 22.9 %copy-start.1 = (f32[4,1,24,48,48]{3,4,2,1,0:T(8,128)}, f32[4,1,24,48,48]{3,4,2,1,0:T(8,128)S(1)}, u32[]{:S(2)}) copy-start(f32[4,1,24,48,48]{3,4,2,1,0:T(8,128)S(1)} %get-tuple-element.1080) | copy-start | bytes 2654212 | tf_op jit(solution)/shard_map/while
  599.6 35.9 %all-gather.12.cloned.1.call-start = ((), (), s32[]{:S(2)}) async-start(), calls=%async_computation.1 | async-start | bytes 1474560 | tf_op jit(solution)/shard_map/while/body/eval_jaxpr/all_gather | solution.py:233
  633.3 11.3 %collective-permute-start.1 = (bf16[1,48,3072]{2,1,0:T(8,128)(2,1)S(1)}, bf16[1,48,3072]{2,1,0:T(8,128)(2,1)}, u32[]{:S(2)}, u32[]{:S(2)}) collective-permute-start(bf16[1,48,3072]{2,1,0:T(8,128)(2,1)S(1)} %fusion.109), channel_id=1, source_target_pairs={{4,0},{8,4},{12,8},{5,1},{9,5},{13,9},{6,2},{10,6},{14,10},{7,3},{... | collective-permute-start | bytes 884744 | tf_op jit(solution)/shard_map/while/body/eval_jaxpr/ppermute | solution.py:40
  652.8 8.4 %collective-permute-start.8 = (bf16[3,48,384]{2,1,0:T(8,128)(2,1)S(1)}, bf16[3,48,384]{2,1,0:T(8,128)(2,1)S(1)}, u32[]{:S(2)}, u32[]{:S(2)}) collective-permute-start(bf16[3,48,384]{2,1,0:T(8,128)(2,1)S(1)} %get-tuple-element.769), channel_id=1, source_target_pairs={{0,1},{1,2},{2,3},{3,0},{4,5},{5,6},{6,7},{7,4},{8,9},{9,10},{10,1... | collective-permute-start | bytes 331784 | tf_op jit(solution)/shard_map/ppermute | solution.py:166
  653.2 8.9 %collective-permute-start.9 = (bf16[3,48,384]{2,1,0:T(8,128)(2,1)S(1)}, bf16[3,48,384]{2,1,0:T(8,128)(2,1)S(1)}, u32[]{:S(2)}, u32[]{:S(2)}) collective-permute-start(bf16[3,48,384]{2,1,0:T(8,128)(2,1)S(1)} %get-tuple-element.768), channel_id=1, source_target_pairs={{0,2},{1,3},{2,0},{3,1},{4,6},{5,7},{6,4},{7,5},{8,10},{9,11},{10,... | collective-permute-start | bytes 331784 | tf_op jit(solution)/shard_map/ppermute | solution.py:166
  661.2 3.2 collective-permute-start.10
  (38 other events, 214.8 us)
Sparse Core Ops, SparseCore 0:
  9.6 113.8 all-gather.9
  374.2 22.8 all-gather.11
  421.1 20.8 all-gather.11
  467.0 19.3 all-gather.11
  512.0 19.3 all-gather.11
  557.0 19.3 all-gather.11
  601.9 19.4 all-gather.11
